TPU v7x, 32 devices: a whole 2x2x4 slice. The times are simulated.
32 devices in a mesh: row: 8 (over y, x, core), col: 4 (over z).
Axes of the slice: x: 2, y: 2, z: 4, core: 2. Of those that a mesh axis runs over, the one named last changes fastest.
Arguments:
- positions: float32 [3, 32768], P(None, ('row', 'col')), may hold values from 0 to 1
- segments: float32 [3, 32768], P(None, ('row', 'col')), may hold values from -1.2 to 1.2
- radius: float32 [32768], P(('row', 'col')), may hold values from 0.05 to 0.2
- currents: float32 [2, 32768], P(None, ('row', 'col')), may hold values from -6 to 6
- resist: float32 [32768], P(('row', 'col')), may hold values from 0.3 to 3
- slot_of: int32 [32768], P(('row', 'col')), may hold values from 0 to 1023, as said below
- pair_list: int32 [1024, 2], P(('row', 'col')), may hold values from 0 to 63, as said below
- near_flag: int32 [1024], P(('row', 'col')), may hold values from 0 to 2, as said below
Outputs:
- voltage: float32 [2, 32768], P(None, ('row', 'col'))
Inputs may be any that keep to these rules, and one draw needn't show every extreme that they name: `slot_of`: the elements of shard d hold the values 0 to 1023 once each; a value s puts the element in cluster d * 2 + s // 512. `pair_list`: shard d = r * 4 + c lists 32 slots; each live slot holds a pair (I, J) with I <= J, I in clusters r * 2 * 4 to (r + 1) * 2 * 4 - 1 and (J // 2) % 4 = c; a pair stands in one live slot at most, over all shards. Empty slots hold I = r * 2 * 4 and J = c * 2. `near_flag`: 0 marks an empty slot.
All inputs are finite; a program needn't handle non-finite values.
Results may differ from a plain program's by a relative error of at most 0.0003.
Values sent between devices are 32-bit elements; how exact they have to be, the bound alone decides.
A program may use at most 64 MiB of HBM per device.

v0:
```python
import math
import jax
import jax.numpy as jnp
from jax import lax
from jax.sharding import PartitionSpec as P

CS = 512
gauss_step = 0.5 / math.sqrt(3.0)
kernel_gain = 0.25
group_size = 4


def partner(block, axis, distance):
    count = lax.axis_size(axis)
    route = []
    for low in range(count):
        high = low | 1 << distance
        if high != low and high < count:
            route += [(low, high), (high, low)]
    return lax.ppermute(block, axis, route)


def tile_block(
    points_first, vectors_first, radii_first, points_second, vectors_second, radii_second, is_near
):
    softening = radii_first[:, None] ** 2 + radii_second[None, :] ** 2
    alignment = vectors_first[0][:, None] * vectors_second[0][None, :]
    for component in (1, 2):
        alignment = (
            alignment + vectors_first[component][:, None] * vectors_second[component][None, :]
        )

    def far_part():
        squared = softening
        for component in range(3):
            squared = (
                squared
                + (points_first[component][:, None] - points_second[component][None, :]) ** 2
            )
        return 1.0 / jnp.sqrt(squared)

    def near_part():
        summed = jnp.zeros_like(softening)
        for sign_first in (-1.0, 1.0):
            for sign_second in (-1.0, 1.0):
                squared = softening
                for component in range(3):
                    moved_first = (
                        points_first[component] + sign_first * gauss_step * vectors_first[component]
                    )
                    moved_second = (
                        points_second[component]
                        + sign_second * gauss_step * vectors_second[component]
                    )
                    squared = squared + (moved_first[:, None] - moved_second[None, :]) ** 2
                summed = summed + 1.0 / jnp.sqrt(squared)
        return 0.25 * summed

    inverse = lax.cond(is_near, near_part, far_part)
    return kernel_gain * alignment * inverse


def slot_terms(block_first, block_second, flag_value, diagonal_pair):
    step_rows = min(128, CS)

    def live_terms():
        is_near = flag_value == 2
        rows_out = []
        mirror_sum = jnp.zeros((2, CS), jnp.float32)
        for offset in range(0, CS, step_rows):
            portion = block_first[:, offset : offset + step_rows]
            kernel_tile = tile_block(
                portion[0:3],
                portion[3:6],
                portion[6],
                block_second[0:3],
                block_second[3:6],
                block_second[6],
                is_near,
            )
            rows_out.append(
                jnp.dot(block_second[7:9], kernel_tile.T, precision=lax.Precision.HIGHEST)
            )
            mirror_sum = mirror_sum + jnp.dot(
                portion[7:9], kernel_tile, precision=lax.Precision.HIGHEST
            )
        mirror_weight = 1.0 - diagonal_pair.astype(jnp.float32)
        return (jnp.concatenate(rows_out, 1), mirror_weight * mirror_sum)

    def empty_terms():
        blank = jnp.zeros((2, CS), jnp.float32)
        return (blank, blank)

    return lax.cond(flag_value > 0, live_terms, empty_terms)


def on_device(positions, segments, radius, currents, resist, slot_of, pair_list, near_flag):
    local_count = positions.shape[1]
    packed = jnp.concatenate([positions, segments, radius[None, :], currents], 0)
    ordered = jnp.zeros_like(packed).at[:, slot_of].set(packed)
    row_block = lax.all_gather(ordered, "col", axis=1, tiled=True)
    col_block = lax.all_gather(ordered, "row", axis=1, tiled=True)
    col_count = lax.axis_size("col")
    row_count = lax.axis_size("row")
    row_pos = lax.axis_index("row")
    per_device = local_count // CS
    row_span = per_device * col_count
    col_span = per_device * row_count
    slot_count = pair_list.shape[0]
    local_first = pair_list[:, 0] - row_pos * row_span
    local_second = pair_list[:, 1] // row_span * per_device + pair_list[:, 1] % per_device
    diagonal_all = (pair_list[:, 0] == pair_list[:, 1]).astype(jnp.int32)

    def add_terms(sums_pair, slot_index, direct_part, mirror_part):
        row_sum, col_sum = sums_pair
        first_id = local_first[slot_index]
        second_id = local_second[slot_index]
        current = lax.dynamic_slice_in_dim(row_sum, first_id * CS, CS, 1)
        row_sum = lax.dynamic_update_slice_in_dim(row_sum, current + direct_part, first_id * CS, 1)
        current = lax.dynamic_slice_in_dim(col_sum, second_id * CS, CS, 1)
        col_sum = lax.dynamic_update_slice_in_dim(col_sum, current + mirror_part, second_id * CS, 1)
        return (row_sum, col_sum)

    row_start = jnp.zeros((2, row_span * CS), jnp.float32)
    col_start = jnp.zeros((2, col_span * CS), jnp.float32)
    half_count = slot_count // 2

    def visit_group(group_index, sums_now):
        for inner in range(group_size):
            slot_index = group_index * group_size + inner
            block_first = lax.dynamic_slice_in_dim(row_block, local_first[slot_index] * CS, CS, 1)
            block_second = lax.dynamic_slice_in_dim(col_block, local_second[slot_index] * CS, CS, 1)
            direct_part, mirror_part = slot_terms(
                block_first, block_second, near_flag[slot_index], diagonal_all[slot_index] > 0
            )
            sums_now = add_terms(sums_now, slot_index, direct_part, mirror_part)
        return sums_now

    row_sum, col_sum = lax.fori_loop(
        0, half_count // group_size, visit_group, (row_start, col_start)
    )
    row_tiles = row_block.reshape(9, row_span, CS)
    col_tiles = col_block.reshape(9, col_span, CS)
    lent_first = jnp.take(row_tiles, local_first[half_count:], axis=1)
    lent_second = jnp.take(col_tiles, local_second[half_count:], axis=1)
    lent_blocks = jnp.concatenate([lent_first, lent_second], 0)
    lent_codes = (near_flag[half_count:] + 3 * diagonal_all[half_count:]).astype(jnp.float32)
    top_bit = lax.axis_size("row").bit_length() - 2
    borrowed_blocks, borrowed_codes = partner((lent_blocks, lent_codes), "row", top_bit)

    def help_group(group_index, results):
        for inner in range(group_size):
            item = group_index * group_size + inner
            block_pair = lax.dynamic_index_in_dim(borrowed_blocks, item, 1, keepdims=False)
            code_value = borrowed_codes[item].astype(jnp.int32)
            direct_part, mirror_part = slot_terms(
                block_pair[0:9], block_pair[9:18], code_value % 3, code_value // 3 > 0
            )
            both_parts = jnp.stack([direct_part, mirror_part])[:, :, None, :]
            results = lax.dynamic_update_slice(results, both_parts, (0, 0, item, 0))
        return results

    helped = lax.fori_loop(
        0, half_count // group_size, help_group, jnp.zeros((2, 2, half_count, CS), jnp.float32)
    )
    returned = partner(helped, "row", top_bit)
    row_sum = (
        row_sum.reshape(2, row_span, CS)
        .at[:, local_first[half_count:], :]
        .add(returned[0])
        .reshape(2, row_span * CS)
    )
    col_sum = (
        col_sum.reshape(2, col_span, CS)
        .at[:, local_second[half_count:], :]
        .add(returned[1])
        .reshape(2, col_span * CS)
    )
    owned = lax.psum_scatter(row_sum, "col", scatter_dimension=1, tiled=True) + lax.psum_scatter(
        col_sum, "row", scatter_dimension=1, tiled=True
    )
    induced = owned[:, slot_of]
    voltage_real = resist * currents[0] - induced[1]
    voltage_imag = resist * currents[1] + induced[0]
    return jnp.stack([voltage_real, voltage_imag])


def solution(mesh):
    return jax.shard_map(
        on_device,
        mesh=mesh,
        in_specs=(
            P(None, ("row", "col")),
            P(None, ("row", "col")),
            P(("row", "col")),
            P(None, ("row", "col")),
            P(("row", "col")),
            P(("row", "col")),
            P(("row", "col"), None),
            P(("row", "col")),
        ),
        out_specs=P(None, ("row", "col")),
        check_vma=False,
    )
```

profile of v0, /device:TPU:0, one launch (start us, length us, event | category | flops | bytes accessed | tf_op | source)
XLA Modules:
  0.0 470.7 jit_solution(10847752534651488676)
XLA Ops:
  6.5 0.7 broadcast_clamp_fusion
  7.2 0.8 maximum_bitcast_fusion.8
  8.3 3.2 scatter_custom_fusion
  11.5 39.7 %all_gather.7 = f32[9,4096]{0,1:T(8,128)S(1)} all-gather(f32[9,1024]{0,1:T(8,128)S(1)} %scatter_custom_fusion), channel_id=1, replica_groups=mesh['row'=8,'col'=4] {'col'}, dimensions={1}, use_global_device_ids=true | all-gather | bytes 184320 | tf_op jit(solution)/shard_map/all_gather | solution.py:101
  51.2 24.6 %all_gather.6 = f32[9,8192]{0,1:T(8,128)} all-gather(f32[9,1024]{0,1:T(8,128)S(1)} %scatter_custom_fusion), channel_id=1, replica_groups=mesh['row'=8,'col'=4] {'row'}, dimensions={1}, use_global_device_ids=true | all-gather | bytes 331776 | tf_op jit(solution)/shard_map/all_gather | solution.py:102
  76.6 2.9 copy.23
  80.0 1.4 gather_fusion.1
  81.5 1.2 select_bitcast_fusion
  83.3 2.0 collective-permute-start
  85.9 2.9 copy.20
  88.8 10.1 %collective-permute-done.1 = f32[18,16,512]{2,1,0:T(8,128)} collective-permute-done((f32[18,16,512]{2,1,0:T(8,128)S(1)}, f32[18,16,512]{2,1,0:T(8,128)}, u32[]{:S(2)}, u32[]{:S(2)}) %collective-permute-start.1) | collective-permute-done | bytes 589856 | tf_op jit(solution)/shard_map/ppermute | solution.py:20
  98.9 1.4 copy.25
  100.4 50.1 %while.34 = (s32[]{:T(128)}, f32[2,2,16,512]{3,1,0,2:T(2,128)S(1)}, f32[16]{0:T(128)S(1)}, f32[18,16,512]{2,0,1:T(8,128)S(1)}, s32[]{:T(128)}, /*index=5*/s32[]{...) while((s32[]{:T(128)}, f32[2,2,16,512]{3,1,0,2:T(2,128)S(1)}, ...), condition=%wide.region_84.85_spmd, body=%wide.region_43.84_spmd.sunk | while | flops 108167224 | bytes 22711308 | solution.py:163
  104.0 4.5 conditional.54
  108.5 4.5 conditional.53
  116.4 4.4 conditional.55
  120.9 4.5 conditional.53
  125.4 4.5 conditional.52
  133.3 4.4 conditional.55
  141.4 4.4 conditional.55
  145.9 4.5 conditional.52
  150.5 39.8 %collective-permute-start.2 = (f32[2,2,16,512]{3,1,0,2:T(2,128)S(1)}, f32[2,2,16,512]{3,1,0,2:T(2,128)S(1)}, u32[]{:S(2)}, u32[]{:S(2)}) collective-permute-start(f32[2,2,16,512]{3,1,0,2:T(2,128)S(1)} %get-tuple-element.1886), channel_id=1, source_target_pairs={{0,16},{16,0},{4,20},{20,4},{8,24},{24,8},{12,28},{28,12},{1,17},{... | collective-permute-start | bytes 393224 | tf_op jit(solution)/shard_map/ppermute | solution.py:20
  190.4 168.9 %while.33 = (s32[]{:T(128)}, f32[2,4096]{1,0:T(2,128)S(1)}, f32[2,8192]{1,0:T(2,128)S(1)}, s32[32]{0:T(128)S(1)}, s32[32]{0:T(128)S(1)}, /*index=5*/s32[32]{0:T(...) while((s32[]{:T(128)}, f32[2,4096]{1,0:T(2,128)S(1)}, ...), condition=%wide.region_42.43_spmd, body=%wide.region_1.42_spmd.sunk | while | flops 108167248 | bytes 22744584 | solution.py:139
  214.1 6.7 %conditional.51 = (f32[2,512]{1,0:T(2,128)S(1)}, f32[2,512]{1,0:T(2,128)S(1)}) conditional(s32[]{:T(128)} %convert_element_type.265, () %tuple.1090, (f32[9,8192]{1,0:T(8,128)S(1)}, s32[]{:T(128)}, f32[9,4096]{1,0:T(8,128)S(1)}, s32[]{:T(128)}, s32[]{:T(128)}, /*index=5*/s32[32]{0:T(128)S(1)}, s32[]{:T(128)}) %tuple.1091), branch_computations={%region_32.32_spmd, %region_33.41_spmd} | conditional | flops 27039756 | bytes 5661272 | solution.py:94
  220.8 6.8 %conditional.50 = (f32[2,512]{1,0:T(2,128)S(1)}, f32[2,512]{1,0:T(2,128)S(1)}) conditional(s32[]{:T(128)} %convert_element_type.264, () %tuple.1088, (f32[9,8192]{1,0:T(8,128)S(1)}, s32[]{:T(128)}, f32[9,4096]{1,0:T(8,128)S(1)}, s32[]{:T(128)}, s32[]{:T(128)}, /*index=5*/s32[32]{0:T(128)S(1)}, s32[]{:T(128)}) %tuple.1089), branch_computations={%region_22.22_spmd, %region_23.31_spmd} | conditional | flops 27039756 | bytes 5661272 | solution.py:94
  227.6 6.8 %conditional.49 = (f32[2,512]{1,0:T(2,128)S(1)}, f32[2,512]{1,0:T(2,128)S(1)}) conditional(s32[]{:T(128)} %convert_element_type.263, () %tuple.1086, (f32[9,8192]{1,0:T(8,128)S(1)}, s32[]{:T(128)}, f32[9,4096]{1,0:T(8,128)S(1)}, s32[]{:T(128)}, s32[]{:T(128)}, /*index=5*/s32[32]{0:T(128)S(1)}, s32[]{:T(128)}) %tuple.1087), branch_computations={%region_12.12_spmd, %region_13.21_spmd} | conditional | flops 27039756 | bytes 5661272 | solution.py:94
  234.4 8.2 %conditional.48 = (f32[2,512]{1,0:T(2,128)S(1)}, f32[2,512]{1,0:T(2,128)S(1)}) conditional(s32[]{:T(128)} %convert_element_type.262, () %tuple.1084, (f32[9,8192]{1,0:T(8,128)S(1)}, s32[]{:T(128)}, f32[9,4096]{1,0:T(8,128)S(1)}, s32[]{:T(128)}, s32[]{:T(128)}, /*index=5*/s32[32]{0:T(128)S(1)}, s32[]{:T(128)}) %tuple.1085), branch_computations={%region_2.2_spmd, %region_3.11_spmd} | conditional | flops 27039756 | bytes 5661272 | solution.py:94
  246.0 0.7 fusion.709
  252.4 8.1 %conditional.51 = (f32[2,512]{1,0:T(2,128)S(1)}, f32[2,512]{1,0:T(2,128)S(1)}) conditional(s32[]{:T(128)} %convert_element_type.265, () %tuple.1090, (f32[9,8192]{1,0:T(8,128)S(1)}, s32[]{:T(128)}, f32[9,4096]{1,0:T(8,128)S(1)}, s32[]{:T(128)}, s32[]{:T(128)}, /*index=5*/s32[32]{0:T(128)S(1)}, s32[]{:T(128)}) %tuple.1091), branch_computations={%region_32.32_spmd, %region_33.41_spmd} | conditional | flops 27039756 | bytes 5661272 | solution.py:94
  260.5 6.8 %conditional.50 = (f32[2,512]{1,0:T(2,128)S(1)}, f32[2,512]{1,0:T(2,128)S(1)}) conditional(s32[]{:T(128)} %convert_element_type.264, () %tuple.1088, (f32[9,8192]{1,0:T(8,128)S(1)}, s32[]{:T(128)}, f32[9,4096]{1,0:T(8,128)S(1)}, s32[]{:T(128)}, s32[]{:T(128)}, /*index=5*/s32[32]{0:T(128)S(1)}, s32[]{:T(128)}) %tuple.1089), branch_computations={%region_22.22_spmd, %region_23.31_spmd} | conditional | flops 27039756 | bytes 5661272 | solution.py:94
  267.3 6.8 %conditional.49 = (f32[2,512]{1,0:T(2,128)S(1)}, f32[2,512]{1,0:T(2,128)S(1)}) conditional(s32[]{:T(128)} %convert_element_type.263, () %tuple.1086, (f32[9,8192]{1,0:T(8,128)S(1)}, s32[]{:T(128)}, f32[9,4096]{1,0:T(8,128)S(1)}, s32[]{:T(128)}, s32[]{:T(128)}, /*index=5*/s32[32]{0:T(128)S(1)}, s32[]{:T(128)}) %tuple.1087), branch_computations={%region_12.12_spmd, %region_13.21_spmd} | conditional | flops 27039756 | bytes 5661272 | solution.py:94
  274.1 8.2 %conditional.48 = (f32[2,512]{1,0:T(2,128)S(1)}, f32[2,512]{1,0:T(2,128)S(1)}) conditional(s32[]{:T(128)} %convert_element_type.262, () %tuple.1084, (f32[9,8192]{1,0:T(8,128)S(1)}, s32[]{:T(128)}, f32[9,4096]{1,0:T(8,128)S(1)}, s32[]{:T(128)}, s32[]{:T(128)}, /*index=5*/s32[32]{0:T(128)S(1)}, s32[]{:T(128)}) %tuple.1085), branch_computations={%region_2.2_spmd, %region_3.11_spmd} | conditional | flops 27039756 | bytes 5661272 | solution.py:94
  292.1 8.1 %conditional.51 = (f32[2,512]{1,0:T(2,128)S(1)}, f32[2,512]{1,0:T(2,128)S(1)}) conditional(s32[]{:T(128)} %convert_element_type.265, () %tuple.1090, (f32[9,8192]{1,0:T(8,128)S(1)}, s32[]{:T(128)}, f32[9,4096]{1,0:T(8,128)S(1)}, s32[]{:T(128)}, s32[]{:T(128)}, /*index=5*/s32[32]{0:T(128)S(1)}, s32[]{:T(128)}) %tuple.1091), branch_computations={%region_32.32_spmd, %region_33.41_spmd} | conditional | flops 27039756 | bytes 5661272 | solution.py:94
  300.2 6.8 %conditional.50 = (f32[2,512]{1,0:T(2,128)S(1)}, f32[2,512]{1,0:T(2,128)S(1)}) conditional(s32[]{:T(128)} %convert_element_type.264, () %tuple.1088, (f32[9,8192]{1,0:T(8,128)S(1)}, s32[]{:T(128)}, f32[9,4096]{1,0:T(8,128)S(1)}, s32[]{:T(128)}, s32[]{:T(128)}, /*index=5*/s32[32]{0:T(128)S(1)}, s32[]{:T(128)}) %tuple.1089), branch_computations={%region_22.22_spmd, %region_23.31_spmd} | conditional | flops 27039756 | bytes 5661272 | solution.py:94
  307.0 6.8 %conditional.49 = (f32[2,512]{1,0:T(2,128)S(1)}, f32[2,512]{1,0:T(2,128)S(1)}) conditional(s32[]{:T(128)} %convert_element_type.263, () %tuple.1086, (f32[9,8192]{1,0:T(8,128)S(1)}, s32[]{:T(128)}, f32[9,4096]{1,0:T(8,128)S(1)}, s32[]{:T(128)}, s32[]{:T(128)}, /*index=5*/s32[32]{0:T(128)S(1)}, s32[]{:T(128)}) %tuple.1087), branch_computations={%region_12.12_spmd, %region_13.21_spmd} | conditional | flops 27039756 | bytes 5661272 | solution.py:94
  313.8 8.2 %conditional.48 = (f32[2,512]{1,0:T(2,128)S(1)}, f32[2,512]{1,0:T(2,128)S(1)}) conditional(s32[]{:T(128)} %convert_element_type.262, () %tuple.1084, (f32[9,8192]{1,0:T(8,128)S(1)}, s32[]{:T(128)}, f32[9,4096]{1,0:T(8,128)S(1)}, s32[]{:T(128)}, s32[]{:T(128)}, /*index=5*/s32[32]{0:T(128)S(1)}, s32[]{:T(128)}) %tuple.1085), branch_computations={%region_2.2_spmd, %region_3.11_spmd} | conditional | flops 27039756 | bytes 5661272 | solution.py:94
  331.7 6.7 %conditional.51 = (f32[2,512]{1,0:T(2,128)S(1)}, f32[2,512]{1,0:T(2,128)S(1)}) conditional(s32[]{:T(128)} %convert_element_type.265, () %tuple.1090, (f32[9,8192]{1,0:T(8,128)S(1)}, s32[]{:T(128)}, f32[9,4096]{1,0:T(8,128)S(1)}, s32[]{:T(128)}, s32[]{:T(128)}, /*index=5*/s32[32]{0:T(128)S(1)}, s32[]{:T(128)}) %tuple.1091), branch_computations={%region_32.32_spmd, %region_33.41_spmd} | conditional | flops 27039756 | bytes 5661272 | solution.py:94
  338.5 6.8 %conditional.50 = (f32[2,512]{1,0:T(2,128)S(1)}, f32[2,512]{1,0:T(2,128)S(1)}) conditional(s32[]{:T(128)} %convert_element_type.264, () %tuple.1088, (f32[9,8192]{1,0:T(8,128)S(1)}, s32[]{:T(128)}, f32[9,4096]{1,0:T(8,128)S(1)}, s32[]{:T(128)}, s32[]{:T(128)}, /*index=5*/s32[32]{0:T(128)S(1)}, s32[]{:T(128)}) %tuple.1089), branch_computations={%region_22.22_spmd, %region_23.31_spmd} | conditional | flops 27039756 | bytes 5661272 | solution.py:94
  345.3 6.8 %conditional.49 = (f32[2,512]{1,0:T(2,128)S(1)}, f32[2,512]{1,0:T(2,128)S(1)}) conditional(s32[]{:T(128)} %convert_element_type.263, () %tuple.1086, (f32[9,8192]{1,0:T(8,128)S(1)}, s32[]{:T(128)}, f32[9,4096]{1,0:T(8,128)S(1)}, s32[]{:T(128)}, s32[]{:T(128)}, /*index=5*/s32[32]{0:T(128)S(1)}, s32[]{:T(128)}) %tuple.1087), branch_computations={%region_12.12_spmd, %region_13.21_spmd} | conditional | flops 27039756 | bytes 5661272 | solution.py:94
  352.1 6.8 %conditional.48 = (f32[2,512]{1,0:T(2,128)S(1)}, f32[2,512]{1,0:T(2,128)S(1)}) conditional(s32[]{:T(128)} %convert_element_type.262, () %tuple.1084, (f32[9,8192]{1,0:T(8,128)S(1)}, s32[]{:T(128)}, f32[9,4096]{1,0:T(8,128)S(1)}, s32[]{:T(128)}, s32[]{:T(128)}, /*index=5*/s32[32]{0:T(128)S(1)}, s32[]{:T(128)}) %tuple.1085), branch_computations={%region_2.2_spmd, %region_3.11_spmd} | conditional | flops 27039756 | bytes 5661272 | solution.py:94
  359.3 1.2 scatter_fusion
  360.5 2.0 copy.26
  362.6 1.2 scatter_fusion.1
  363.8 2.7 copy.27
  366.6 38.1 %reduce-scatter.3.cloned.1.call-done = f32[2,1024]{0,1:T(8,128)} async-done(((f32[2,4096]{0,1:T(8,128)}), f32[2,1024]{0,1:T(8,128)}) %reduce-scatter.3.cloned.1.call-update) | async-done | bytes 8208 | tf_op jit(solution)/shard_map/reduce_scatter | solution.py:179
  404.7 53.7 %reduce-scatter.5.cloned.1.call-done = f32[2,1024]{0,1:T(8,128)} async-done(((f32[2,8192]{0,1:T(8,128)}), f32[2,1024]{0,1:T(8,128)}) %reduce-scatter.5.cloned.1.call-update) | async-done | bytes 8208 | tf_op jit(solution)/shard_map/reduce_scatter | solution.py:179
  458.5 1.3 add.6301
  459.7 2.8 gather_fusion.2
  (879 shorter events, 166.3 us)
Async XLA Ops:
  6.5 398.2 %reduce-scatter.3.cloned.1.call-start = ((), (), s32[]{:S(2)}) async-start(), calls=%async_computation.2 | async-start | bytes 2621440 | tf_op jit(solution)/shard_map/reduce_scatter | solution.py:179
  8.0 67.7 %copy-start.3 = (s32[32,2]{0,1:T(2,128)S(1)}, s32[32,2]{0,1:T(2,128)}, u32[]{:S(2)}) copy-start(s32[32,2]{0,1:T(2,128)} %param.98) | copy-start | bytes 772
  79.4 3.8 copy-start
  83.1 15.8 %collective-permute-start.1 = (f32[18,16,512]{2,1,0:T(8,128)S(1)}, f32[18,16,512]{2,1,0:T(8,128)}, u32[]{:S(2)}, u32[]{:S(2)}) collective-permute-start(f32[18,16,512]{2,1,0:T(8,128)S(1)} %copy.24), channel_id=1, source_target_pairs={{0,16},{16,0},{4,20},{20,4},{8,24},{24,8},{12,28},{28,12},{1,17},{... | collective-permute-start | bytes 1769480 | tf_op jit(solution)/shard_map/ppermute | solution.py:20
  83.3 17.0 %collective-permute-start = (f32[16]{0:T(128)S(1)}, f32[16]{0:T(128)S(1)}, u32[]{:S(2)}, u32[]{:S(2)}) collective-permute-start(f32[16]{0:T(128)S(1)} %add_convert_fusion), channel_id=1, source_target_pairs={{0,16},{16,0},{4,20},{20,4},{8,24},{24,8},{12,28},{28,12},{1,17},{... | collective-permute-start | bytes 200 | tf_op jit(solution)/shard_map/ppermute | solution.py:20
  150.5 208.8 %collective-permute-start.2 = (f32[2,2,16,512]{3,1,0,2:T(2,128)S(1)}, f32[2,2,16,512]{3,1,0,2:T(2,128)S(1)}, u32[]{:S(2)}, u32[]{:S(2)}) collective-permute-start(f32[2,2,16,512]{3,1,0,2:T(2,128)S(1)} %get-tuple-element.1886), channel_id=1, source_target_pairs={{0,16},{16,0},{4,20},{20,4},{8,24},{24,8},{12,28},{28,12},{1,17},{... | collective-permute-start | bytes 393224 | tf_op jit(solution)/shard_map/ppermute | solution.py:20
  362.6 95.9 %reduce-scatter.5.cloned.1.call-start = ((), (), s32[]{:S(2)}) async-start(), calls=%async_computation.3 | async-start | bytes 4718592 | tf_op jit(solution)/shard_map/reduce_scatter | solution.py:179
  363.8 2.8 copy-start.1
  366.6 96.5 %copy-start.2 = (f32[1024]{0:T(1024)S(1)}, f32[1024]{0:T(1024)}, u32[]{:S(2)}) copy-start(f32[1024]{0:T(1024)} %param.96) | copy-start | bytes 12292
Sparse Core Ops, SparseCore 0:
  362.7 41.9 reduce-scatter.2
  408.1 50.3 reduce-scatter.4
where the time goes:
time: 476 us; the launch traced here: 471 us
  waiting for transfers between devices  102 us (21%)
  loops' own time  83.9 us (18%)
  matrix products  77.9 us (16%)
  blocking collectives  64.3 us (14%)
  local copies, waits for them, and re-layouts  48.4 us (10%)
  starting transfers between devices  41.9 us (9%)
  other arithmetic  38.4 us (8%)
  between operations  13.9 us (3%)
    reduce_scatter x1, waiting for transfers between devices, on_device(): lax.psum_scatter(col_sum, 'row', scatter_dimension=1, tiled=True)  53.7 us
    another operation x1, loops' own time, on_device(): lax.fori_loop(0, half_count // group_size, visit_group, (row_start, col_s...  45 us
    ppermute x3, starting transfers between devices, partner(): return lax.ppermute(block, axis, route)  41.9 us
    dot_general x96, matrix products, live_terms(): jnp.dot(block_second[7:9], kernel_tile.T, precision=lax.Precision.HIGHEST)  40.9 us
    all_gather x1, blocking collectives, on_device(): row_block = lax.all_gather(ordered, 'col', axis=1, tiled=True)  39.7 us
    reduce_scatter x1, waiting for transfers between devices, on_device(): lax.psum_scatter(row_sum, 'col', scatter_dimension=1, tiled=True)  38.1 us
    dot_general x96, matrix products, live_terms(): jnp.dot(portion[7:9], kernel_tile, precision=lax.Precision.HIGHEST)  37 us
    all_gather x1, blocking collectives, on_device(): col_block = lax.all_gather(ordered, 'row', axis=1, tiled=True)  24.6 us
  transfers between devices with their start and end apart: 5, of which 3 were waited for; matrix products, arithmetic and copies ran while one was open for 23% of the time, Pallas kernels for 0%

commit v1 on v0

--- a/solution.py
+++ b/solution.py
@@ -99,7 +99,14 @@
     packed = jnp.concatenate([positions, segments, radius[None, :], currents], 0)
     ordered = jnp.zeros_like(packed).at[:, slot_of].set(packed)
     row_block = lax.all_gather(ordered, "col", axis=1, tiled=True)
-    col_block = lax.all_gather(ordered, "row", axis=1, tiled=True)
+    ways, here = (lax.axis_size("row"), lax.axis_index("row"))
+    col_block, reach = (ordered, 1)
+    while reach < ways:
+        theirs = lax.ppermute(col_block, "row", [(d, d ^ reach) for d in range(ways)])
+        mine_first = jnp.concatenate([col_block, theirs], axis=1)
+        theirs_first = jnp.concatenate([theirs, col_block], axis=1)
+        col_block = jnp.where(here & reach == 0, mine_first, theirs_first)
+        reach = 2 * reach
     col_count = lax.axis_size("col")
     row_count = lax.axis_size("row")
     row_pos = lax.axis_index("row")

time: 476 us -> 460 us (0.966)
  blocking collectives: 64.3 us -> 38.5 us
  waiting for transfers between devices: 102 us -> 112 us
    all_gather x1 -> x0, blocking collectives: 24.6 us -> none  [on_device(): col_block = lax.all_gather(ordered, 'row', axis=1, tiled=True)]
    ppermute x0 -> x3, waiting for transfers between devices: none -> 8.39 us  [on_device(): lax.ppermute(col_block, 'row', [(d, d ^ reach) for d in range(ways)])]
  transfers between devices with their start and end apart: 5 -> 8, of which waited for: 3 -> 5; matrix products, arithmetic and copies ran while one was open for 23% -> 25% of each run, Pallas kernels for 0% -> 0%
where the time goes in v1:
time: 460 us; the launch traced here: 455 us
  waiting for transfers between devices  112 us (24%)
  loops' own time  82.1 us (18%)
  matrix products  76.5 us (17%)
  starting transfers between devices  45.4 us (10%)
  local copies, waits for them, and re-layouts  44.5 us (10%)
  other arithmetic  41.8 us (9%)
  blocking collectives  38.5 us (8%)
  between operations  14 us (3%)
    reduce_scatter x1, waiting for transfers between devices, on_device(): lax.psum_scatter(col_sum, 'row', scatter_dimension=1, tiled=True)  53.8 us
    another operation x1, loops' own time, on_device(): lax.fori_loop(0, half_count // group_size, visit_group, (row_start, col_s...  44.3 us
    ppermute x3, starting transfers between devices, partner(): return lax.ppermute(block, axis, route)  42.6 us
    dot_general x96, matrix products, live_terms(): jnp.dot(block_second[7:9], kernel_tile.T, precision=lax.Precision.HIGHEST)  41 us
    all_gather x1, blocking collectives, on_device(): row_block = lax.all_gather(ordered, 'col', axis=1, tiled=True)  38.5 us
    reduce_scatter x1, waiting for transfers between devices, on_device(): lax.psum_scatter(row_sum, 'col', scatter_dimension=1, tiled=True)  38.3 us
    dot_general x96, matrix products, live_terms(): jnp.dot(portion[7:9], kernel_tile, precision=lax.Precision.HIGHEST)  35.5 us
    another operation x32, loops' own time, slot_terms(): return lax.cond(flag_value > 0, live_terms, empty_terms)  24.6 us
  transfers between devices with their start and end apart: 8, of which 5 were waited for; matrix products, arithmetic and copies ran while one was open for 25% of the time, Pallas kernels for 0%

profile of v1, /device:TPU:0, one launch (start us, length us, event | category | flops | bytes accessed | tf_op | source)
XLA Modules:
  0.0 454.7 jit_solution(4925731637553334860)
XLA Ops:
  6.5 0.7 broadcast_clamp_fusion
  7.2 0.8 maximum_bitcast_fusion.8
  8.3 3.2 scatter_custom_fusion
  12.0 0.8 compare_convert_fusion
  12.8 1.3 add_convert_fusion
  14.1 2.5 collective-permute-start.3
  18.9 38.5 %all_gather.3 = f32[9,4096]{0,1:T(8,128)S(1)} all-gather(f32[9,1024]{0,1:T(8,128)S(1)} %scatter_custom_fusion), channel_id=1, replica_groups=mesh['row'=8,'col'=4] {'col'}, dimensions={1}, use_global_device_ids=true | all-gather | bytes 184320 | tf_op jit(solution)/shard_map/all_gather | solution.py:101
  58.0 1.3 copy.47
  59.3 1.6 gather_fusion
  61.2 1.6 collective-permute-start.1
  63.6 2.7 collective-permute-done.1
  67.0 5.7 %collective-permute-done.2 = f32[9,4096]{1,0:T(8,128)S(1)} collective-permute-done((f32[9,4096]{1,0:T(8,128)S(1)}, f32[9,4096]{1,0:T(8,128)S(1)}, u32[]{:S(2)}, u32[]{:S(2)}) %collective-permute-start.2) | collective-permute-done | bytes 147488 | tf_op jit(solution)/shard_map/ppermute | solution.py:105
  74.9 11.5 %collective-permute-done.4 = f32[18,16,512]{2,1,0:T(8,128)S(1)} collective-permute-done((f32[18,16,512]{2,1,0:T(8,128)S(1)}, f32[18,16,512]{2,1,0:T(8,128)S(1)}, u32[]{:S(2)}, u32[]{:S(2)}) %collective-permute-start.4) | collective-permute-done | bytes 589856 | tf_op jit(solution)/shard_map/ppermute | solution.py:20
  86.9 49.0 %while.34 = (s32[]{:T(128)}, f32[2,2,16,512]{3,1,0,2:T(2,128)S(1)}, f32[16]{0:T(128)S(1)}, f32[18,16,512]{2,0,1:T(8,128)S(1)}, s32[]{:T(128)}, /*index=5*/s32[]{...) while((s32[]{:T(128)}, f32[2,2,16,512]{3,1,0,2:T(2,128)S(1)}, ...), condition=%wide.region_84.85_spmd, body=%wide.region_43.84_spmd.sunk | while | flops 108167224 | bytes 22711308 | solution.py:170
  89.1 4.4 conditional.53
  94.1 4.4 conditional.54
  100.6 4.4 conditional.52
  105.6 4.4 conditional.53
  111.4 4.4 conditional.55
  119.3 4.4 conditional.55
  125.0 4.4 conditional.52
  131.5 4.4 conditional.55
  135.9 39.5 %collective-permute-start.5 = (f32[2,2,16,512]{3,1,0,2:T(2,128)S(1)}, f32[2,2,16,512]{3,1,0,2:T(2,128)S(1)}, u32[]{:S(2)}, u32[]{:S(2)}) collective-permute-start(f32[2,2,16,512]{3,1,0,2:T(2,128)S(1)} %get-tuple-element.1886), channel_id=1, source_target_pairs={{0,16},{16,0},{4,20},{20,4},{8,24},{24,8},{12,28},{28,12},{1,17},{... | collective-permute-start | bytes 393224 | tf_op jit(solution)/shard_map/ppermute | solution.py:20
  175.5 166.8 %while.33 = (s32[]{:T(128)}, f32[2,4096]{1,0:T(2,128)S(1)}, f32[2,8192]{1,0:T(2,128)S(1)}, s32[32]{0:T(128)S(1)}, s32[32]{0:T(128)S(1)}, /*index=5*/s32[32]{0:T(...) while((s32[]{:T(128)}, f32[2,4096]{1,0:T(2,128)S(1)}, ...), condition=%wide.region_42.43_spmd, body=%wide.region_1.42_spmd.sunk | while | flops 108167248 | bytes 22744584 | solution.py:146
  193.5 6.6 %conditional.49 = (f32[2,512]{1,0:T(2,128)S(1)}, f32[2,512]{1,0:T(2,128)S(1)}) conditional(s32[]{:T(128)} %convert_element_type.263, () %tuple.1088, (f32[9,8192]{1,0:T(8,128)S(1)}, s32[]{:T(128)}, f32[9,4096]{1,0:T(8,128)S(1)}, s32[]{:T(128)}, s32[]{:T(128)}, /*index=5*/s32[32]{0:T(128)S(1)}, s32[]{:T(128)}) %tuple.1089), branch_computations={%region_12.12_spmd, %region_13.21_spmd} | conditional | flops 27039756 | bytes 5661272 | solution.py:94
  202.0 8.0 %conditional.48 = (f32[2,512]{1,0:T(2,128)S(1)}, f32[2,512]{1,0:T(2,128)S(1)}) conditional(s32[]{:T(128)} %convert_element_type.262, () %tuple.1086, (f32[9,8192]{1,0:T(8,128)S(1)}, s32[]{:T(128)}, f32[9,4096]{1,0:T(8,128)S(1)}, s32[]{:T(128)}, s32[]{:T(128)}, /*index=5*/s32[32]{0:T(128)S(1)}, s32[]{:T(128)}) %tuple.1087), branch_computations={%region_2.2_spmd, %region_3.11_spmd} | conditional | flops 27039756 | bytes 5661272 | solution.py:94
  211.9 6.7 %conditional.50 = (f32[2,512]{1,0:T(2,128)S(1)}, f32[2,512]{1,0:T(2,128)S(1)}) conditional(s32[]{:T(128)} %convert_element_type.264, () %tuple.1090, (f32[9,8192]{1,0:T(8,128)S(1)}, s32[]{:T(128)}, f32[9,4096]{1,0:T(8,128)S(1)}, s32[]{:T(128)}, s32[]{:T(128)}, /*index=5*/s32[32]{0:T(128)S(1)}, s32[]{:T(128)}) %tuple.1091), branch_computations={%region_22.22_spmd, %region_23.31_spmd} | conditional | flops 27039756 | bytes 5661272 | solution.py:94
  220.6 6.8 %conditional.51 = (f32[2,512]{1,0:T(2,128)S(1)}, f32[2,512]{1,0:T(2,128)S(1)}) conditional(s32[]{:T(128)} %convert_element_type.265, () %tuple.1092, (f32[9,8192]{1,0:T(8,128)S(1)}, s32[]{:T(128)}, f32[9,4096]{1,0:T(8,128)S(1)}, s32[]{:T(128)}, s32[]{:T(128)}, /*index=5*/s32[32]{0:T(128)S(1)}, s32[]{:T(128)}) %tuple.1093), branch_computations={%region_32.32_spmd, %region_33.41_spmd} | conditional | flops 27039756 | bytes 5661272 | solution.py:94
  231.3 6.6 %conditional.49 = (f32[2,512]{1,0:T(2,128)S(1)}, f32[2,512]{1,0:T(2,128)S(1)}) conditional(s32[]{:T(128)} %convert_element_type.263, () %tuple.1088, (f32[9,8192]{1,0:T(8,128)S(1)}, s32[]{:T(128)}, f32[9,4096]{1,0:T(8,128)S(1)}, s32[]{:T(128)}, s32[]{:T(128)}, /*index=5*/s32[32]{0:T(128)S(1)}, s32[]{:T(128)}) %tuple.1089), branch_computations={%region_12.12_spmd, %region_13.21_spmd} | conditional | flops 27039756 | bytes 5661272 | solution.py:94
  239.8 8.0 %conditional.48 = (f32[2,512]{1,0:T(2,128)S(1)}, f32[2,512]{1,0:T(2,128)S(1)}) conditional(s32[]{:T(128)} %convert_element_type.262, () %tuple.1086, (f32[9,8192]{1,0:T(8,128)S(1)}, s32[]{:T(128)}, f32[9,4096]{1,0:T(8,128)S(1)}, s32[]{:T(128)}, s32[]{:T(128)}, /*index=5*/s32[32]{0:T(128)S(1)}, s32[]{:T(128)}) %tuple.1087), branch_computations={%region_2.2_spmd, %region_3.11_spmd} | conditional | flops 27039756 | bytes 5661272 | solution.py:94
  249.7 6.7 %conditional.50 = (f32[2,512]{1,0:T(2,128)S(1)}, f32[2,512]{1,0:T(2,128)S(1)}) conditional(s32[]{:T(128)} %convert_element_type.264, () %tuple.1090, (f32[9,8192]{1,0:T(8,128)S(1)}, s32[]{:T(128)}, f32[9,4096]{1,0:T(8,128)S(1)}, s32[]{:T(128)}, s32[]{:T(128)}, /*index=5*/s32[32]{0:T(128)S(1)}, s32[]{:T(128)}) %tuple.1091), branch_computations={%region_22.22_spmd, %region_23.31_spmd} | conditional | flops 27039756 | bytes 5661272 | solution.py:94
  258.4 8.1 %conditional.51 = (f32[2,512]{1,0:T(2,128)S(1)}, f32[2,512]{1,0:T(2,128)S(1)}) conditional(s32[]{:T(128)} %convert_element_type.265, () %tuple.1092, (f32[9,8192]{1,0:T(8,128)S(1)}, s32[]{:T(128)}, f32[9,4096]{1,0:T(8,128)S(1)}, s32[]{:T(128)}, s32[]{:T(128)}, /*index=5*/s32[32]{0:T(128)S(1)}, s32[]{:T(128)}) %tuple.1093), branch_computations={%region_32.32_spmd, %region_33.41_spmd} | conditional | flops 27039756 | bytes 5661272 | solution.py:94
  270.4 6.6 %conditional.49 = (f32[2,512]{1,0:T(2,128)S(1)}, f32[2,512]{1,0:T(2,128)S(1)}) conditional(s32[]{:T(128)} %convert_element_type.263, () %tuple.1088, (f32[9,8192]{1,0:T(8,128)S(1)}, s32[]{:T(128)}, f32[9,4096]{1,0:T(8,128)S(1)}, s32[]{:T(128)}, s32[]{:T(128)}, /*index=5*/s32[32]{0:T(128)S(1)}, s32[]{:T(128)}) %tuple.1089), branch_computations={%region_12.12_spmd, %region_13.21_spmd} | conditional | flops 27039756 | bytes 5661272 | solution.py:94
  278.9 8.0 %conditional.48 = (f32[2,512]{1,0:T(2,128)S(1)}, f32[2,512]{1,0:T(2,128)S(1)}) conditional(s32[]{:T(128)} %convert_element_type.262, () %tuple.1086, (f32[9,8192]{1,0:T(8,128)S(1)}, s32[]{:T(128)}, f32[9,4096]{1,0:T(8,128)S(1)}, s32[]{:T(128)}, s32[]{:T(128)}, /*index=5*/s32[32]{0:T(128)S(1)}, s32[]{:T(128)}) %tuple.1087), branch_computations={%region_2.2_spmd, %region_3.11_spmd} | conditional | flops 27039756 | bytes 5661272 | solution.py:94
  288.8 6.7 %conditional.50 = (f32[2,512]{1,0:T(2,128)S(1)}, f32[2,512]{1,0:T(2,128)S(1)}) conditional(s32[]{:T(128)} %convert_element_type.264, () %tuple.1090, (f32[9,8192]{1,0:T(8,128)S(1)}, s32[]{:T(128)}, f32[9,4096]{1,0:T(8,128)S(1)}, s32[]{:T(128)}, s32[]{:T(128)}, /*index=5*/s32[32]{0:T(128)S(1)}, s32[]{:T(128)}) %tuple.1091), branch_computations={%region_22.22_spmd, %region_23.31_spmd} | conditional | flops 27039756 | bytes 5661272 | solution.py:94
  297.5 8.1 %conditional.51 = (f32[2,512]{1,0:T(2,128)S(1)}, f32[2,512]{1,0:T(2,128)S(1)}) conditional(s32[]{:T(128)} %convert_element_type.265, () %tuple.1092, (f32[9,8192]{1,0:T(8,128)S(1)}, s32[]{:T(128)}, f32[9,4096]{1,0:T(8,128)S(1)}, s32[]{:T(128)}, s32[]{:T(128)}, /*index=5*/s32[32]{0:T(128)S(1)}, s32[]{:T(128)}) %tuple.1093), branch_computations={%region_32.32_spmd, %region_33.41_spmd} | conditional | flops 27039756 | bytes 5661272 | solution.py:94
  309.6 6.6 %conditional.49 = (f32[2,512]{1,0:T(2,128)S(1)}, f32[2,512]{1,0:T(2,128)S(1)}) conditional(s32[]{:T(128)} %convert_element_type.263, () %tuple.1088, (f32[9,8192]{1,0:T(8,128)S(1)}, s32[]{:T(128)}, f32[9,4096]{1,0:T(8,128)S(1)}, s32[]{:T(128)}, s32[]{:T(128)}, /*index=5*/s32[32]{0:T(128)S(1)}, s32[]{:T(128)}) %tuple.1089), branch_computations={%region_12.12_spmd, %region_13.21_spmd} | conditional | flops 27039756 | bytes 5661272 | solution.py:94
  318.0 6.7 %conditional.48 = (f32[2,512]{1,0:T(2,128)S(1)}, f32[2,512]{1,0:T(2,128)S(1)}) conditional(s32[]{:T(128)} %convert_element_type.262, () %tuple.1086, (f32[9,8192]{1,0:T(8,128)S(1)}, s32[]{:T(128)}, f32[9,4096]{1,0:T(8,128)S(1)}, s32[]{:T(128)}, s32[]{:T(128)}, /*index=5*/s32[32]{0:T(128)S(1)}, s32[]{:T(128)}) %tuple.1087), branch_computations={%region_2.2_spmd, %region_3.11_spmd} | conditional | flops 27039756 | bytes 5661272 | solution.py:94
  326.6 6.7 %conditional.50 = (f32[2,512]{1,0:T(2,128)S(1)}, f32[2,512]{1,0:T(2,128)S(1)}) conditional(s32[]{:T(128)} %convert_element_type.264, () %tuple.1090, (f32[9,8192]{1,0:T(8,128)S(1)}, s32[]{:T(128)}, f32[9,4096]{1,0:T(8,128)S(1)}, s32[]{:T(128)}, s32[]{:T(128)}, /*index=5*/s32[32]{0:T(128)S(1)}, s32[]{:T(128)}) %tuple.1091), branch_computations={%region_22.22_spmd, %region_23.31_spmd} | conditional | flops 27039756 | bytes 5661272 | solution.py:94
  335.3 6.8 %conditional.51 = (f32[2,512]{1,0:T(2,128)S(1)}, f32[2,512]{1,0:T(2,128)S(1)}) conditional(s32[]{:T(128)} %convert_element_type.265, () %tuple.1092, (f32[9,8192]{1,0:T(8,128)S(1)}, s32[]{:T(128)}, f32[9,4096]{1,0:T(8,128)S(1)}, s32[]{:T(128)}, s32[]{:T(128)}, /*index=5*/s32[32]{0:T(128)S(1)}, s32[]{:T(128)}) %tuple.1093), branch_computations={%region_32.32_spmd, %region_33.41_spmd} | conditional | flops 27039756 | bytes 5661272 | solution.py:94
  342.4 1.2 scatter_fusion
  343.6 2.0 copy.58
  345.7 1.2 scatter_fusion.1
  346.9 2.7 copy.59
  350.3 38.3 %reduce-scatter.3.cloned.1.call-done = f32[2,1024]{0,1:T(8,128)} async-done(((f32[2,4096]{0,1:T(8,128)}), f32[2,1024]{0,1:T(8,128)}) %reduce-scatter.3.cloned.1.call-update) | async-done | bytes 8208 | tf_op jit(solution)/shard_map/reduce_scatter | solution.py:186
  388.7 53.8 %reduce-scatter.5.cloned.1.call-done = f32[2,1024]{0,1:T(8,128)} async-done(((f32[2,8192]{0,1:T(8,128)}), f32[2,1024]{0,1:T(8,128)}) %reduce-scatter.5.cloned.1.call-update) | async-done | bytes 8208 | tf_op jit(solution)/shard_map/reduce_scatter | solution.py:186
  442.4 1.3 add.6301
  443.7 2.8 gather_fusion.2
  (911 shorter events, 170.2 us)
Async XLA Ops:
  6.5 10.5 %copy-start.6 = (s32[32,2]{0,1:T(2,128)S(1)}, s32[32,2]{0,1:T(2,128)}, u32[]{:S(2)}) copy-start(s32[32,2]{0,1:T(2,128)} %param.98) | copy-start | bytes 772
  6.5 382.1 %reduce-scatter.3.cloned.1.call-start = ((), (), s32[]{:S(2)}) async-start(), calls=%async_computation.2 | async-start | bytes 2621440 | tf_op jit(solution)/shard_map/reduce_scatter | solution.py:186
  11.5 49.5 %collective-permute-start = (f32[9,1024]{0,1:T(8,128)S(1)}, f32[9,1024]{0,1:T(8,128)S(1)}, u32[]{:S(2)}, u32[]{:S(2)}) collective-permute-start(f32[9,1024]{0,1:T(8,128)S(1)} %scatter_custom_fusion), channel_id=1, source_target_pairs={{0,4},{4,0},{8,12},{12,8},{16,20},{20,16},{24,28},{28,24},{1,5},{5... | collective-permute-start | bytes 110600 | tf_op jit(solution)/shard_map/ppermute | solution.py:105
  12.8 4.9 %copy-start.9 = (s32[32]{0:T(128)}, s32[32]{0:T(128)S(1)}, u32[]{:S(2)}) copy-start(s32[32]{0:T(128)S(1)} %compare_convert_fusion) | copy-start | bytes 388
  14.1 72.7 %collective-permute-start.3 = (f32[16]{0:T(128)}, f32[16]{0:T(128)S(1)}, u32[]{:S(2)}, u32[]{:S(2)}) collective-permute-start(f32[16]{0:T(128)} %add_convert_fusion), channel_id=1, source_target_pairs={{0,16},{16,0},{4,20},{20,4},{8,24},{24,8},{12,28},{28,12},{1,17},{... | collective-permute-start | bytes 200 | tf_op jit(solution)/shard_map/ppermute | solution.py:20
  18.3 0.6 copy-start.4
  61.2 5.0 %collective-permute-start.1 = (f32[9,2048]{1,0:T(8,128)S(1)}, f32[9,2048]{1,0:T(8,128)S(1)}, u32[]{:S(2)}, u32[]{:S(2)}) collective-permute-start(f32[9,2048]{1,0:T(8,128)S(1)} %maximum_select_fusion.4), channel_id=1, source_target_pairs={{0,8},{4,12},{8,0},{12,4},{16,24},{20,28},{24,16},{28,20},{1,9},{5... | collective-permute-start | bytes 221192 | tf_op jit(solution)/shard_map/ppermute | solution.py:105
  66.3 7.4 %copy-start.7 = (pred[16]{0:T(512)(128)(4,1)S(1)}, pred[16]{0:T(512)(128)(4,1)}, u32[]{:S(2)}) copy-start(pred[16]{0:T(512)(128)(4,1)} %get-tuple-element.1962) | copy-start | bytes 52
  66.3 7.4 %copy-start.8 = (pred[16]{0:T(512)(128)(4,1)S(1)}, pred[16]{0:T(512)(128)(4,1)}, u32[]{:S(2)}) copy-start(pred[16]{0:T(512)(128)(4,1)} %get-tuple-element.1960) | copy-start | bytes 52
  66.3 6.4 %collective-permute-start.2 = (f32[9,4096]{1,0:T(8,128)S(1)}, f32[9,4096]{1,0:T(8,128)S(1)}, u32[]{:S(2)}, u32[]{:S(2)}) collective-permute-start(f32[9,4096]{1,0:T(8,128)S(1)} %maximum_select_fusion.2), channel_id=1, source_target_pairs={{0,16},{4,20},{8,24},{12,28},{16,0},{20,4},{24,8},{28,12},{1,17},{... | collective-permute-start | bytes 442376 | tf_op jit(solution)/shard_map/ppermute | solution.py:105
  74.3 12.2 %collective-permute-start.4 = (f32[18,16,512]{2,1,0:T(8,128)S(1)}, f32[18,16,512]{2,1,0:T(8,128)S(1)}, u32[]{:S(2)}, u32[]{:S(2)}) collective-permute-start(f32[18,16,512]{2,1,0:T(8,128)S(1)} %copy.56), channel_id=1, source_target_pairs={{0,16},{16,0},{4,20},{20,4},{8,24},{24,8},{12,28},{28,12},{1,17},{... | collective-permute-start | bytes 1769480 | tf_op jit(solution)/shard_map/ppermute | solution.py:20
  86.9 88.6 %copy-start = (s32[32]{0:T(128)S(1)}, s32[32]{0:T(128)}, u32[]{:S(2)}) copy-start(s32[32]{0:T(128)} %param.99) | copy-start | bytes 388
  86.9 88.6 %copy-start.10 = (s32[32]{0:T(128)S(1)}, s32[32]{0:T(128)}, u32[]{:S(2)}) copy-start(s32[32]{0:T(128)} %copy-done.9) | copy-start | bytes 388
  135.9 206.5 %collective-permute-start.5 = (f32[2,2,16,512]{3,1,0,2:T(2,128)S(1)}, f32[2,2,16,512]{3,1,0,2:T(2,128)S(1)}, u32[]{:S(2)}, u32[]{:S(2)}) collective-permute-start(f32[2,2,16,512]{3,1,0,2:T(2,128)S(1)} %get-tuple-element.1886), channel_id=1, source_target_pairs={{0,16},{16,0},{4,20},{20,4},{8,24},{24,8},{12,28},{28,12},{1,17},{... | collective-permute-start | bytes 393224 | tf_op jit(solution)/shard_map/ppermute | solution.py:20
  175.5 166.9 %copy-start.5 = (s32[16]{0:T(128)S(1)}, s32[16]{0:T(128)}, u32[]{:S(2)}) copy-start(s32[16]{0:T(128)} %copy-done.4) | copy-start | bytes 196
  343.6 2.1 copy-start.3
  345.6 96.8 %reduce-scatter.5.cloned.1.call-start = ((), (), s32[]{:S(2)}) async-start(), calls=%async_computation.3 | async-start | bytes 4718592 | tf_op jit(solution)/shard_map/reduce_scatter | solution.py:186
  349.6 0.7 copy-start.1
  350.3 96.7 %copy-start.2 = (f32[1024]{0:T(1024)S(1)}, f32[1024]{0:T(1024)}, u32[]{:S(2)}) copy-start(f32[1024]{0:T(1024)} %param.96) | copy-start | bytes 12292
Sparse Core Ops, SparseCore 0:
  345.8 42.8 reduce-scatter.2
  392.0 50.3 reduce-scatter.4
